TPU v7x, 32 devices: a whole 2x2x4 slice. The times are simulated.
32 devices in a mesh: dp: 8 (over z, x), tensor: 4 (over y, core).
Axes of the slice: x: 2, y: 2, z: 4, core: 2. Of those that a mesh axis runs over, the one named last changes fastest.
Arguments:
- patches: bfloat16 [192, 196, 768], P('dp'), may hold values from -6 to 6
- keep_slots: int32 [192, 98], P('dp'), may hold values from 0 to 195, as said below
- visible_count: int32 [192], P('dp'), may hold values from 39 to 98, as said below
- gain_one: float32 [768], replicated, may hold values from 0.1 to 1.9
- shift_one: float32 [768], replicated, may hold values from -4 to 4
- w_qkv: bfloat16 [3, 768, 768], P(None, None, 'tensor'), may hold values from -0.21875 to 0.21875
- b_qv: float32 [2, 768], P(None, 'tensor'), may hold values from -4 to 4
- w_out: bfloat16 [768, 768], P('tensor'), may hold values from -1.75 to 1.75
- b_out: float32 [768], replicated, may hold values from -4 to 4
- gain_two: float32 [768], replicated, may hold values from 0.1 to 1.9
- shift_two: float32 [768], replicated, may hold values from -4 to 4
- w_fc1: bfloat16 [768, 3072], P(None, 'tensor'), may hold values from -0.21875 to 0.21875
- b_fc1: float32 [3072], P('tensor'), may hold values from -4 to 4
- w_fc2: bfloat16 [3072, 768], P('tensor'), may hold values from -0.109375 to 0.109375
- b_fc2: float32 [768], replicated, may hold values from -4 to 4
- out_grad: bfloat16 [192, 98, 768], P(('dp', 'tensor')), may hold values from -6 to 6
Outputs:
- layer_out: bfloat16 [192, 98, 768], P(('dp', 'tensor'))
- grad_patches: float32 [192, 196, 768], P(('dp', 'tensor'))
- grad_gain_one: float32 [768], replicated
- grad_shift_one: float32 [768], replicated
- grad_w_qkv: float32 [3, 768, 768], P(None, None, 'tensor')
- grad_b_qv: float32 [2, 768], P(None, 'tensor')
- grad_w_out: float32 [768, 768], P('tensor')
- grad_b_out: float32 [768], replicated
- grad_gain_two: float32 [768], replicated
- grad_shift_two: float32 [768], replicated
- grad_w_fc1: float32 [768, 3072], P(None, 'tensor')
- grad_b_fc1: float32 [3072], P('tensor')
- grad_w_fc2: float32 [3072, 768], P('tensor')
- grad_b_fc2: float32 [768], replicated
Inputs may be any that keep to these rules, and one draw needn't show every extreme that they name: `visible_count`: visible patches of each image; in every draw some image has 98 and some has 196 // 5. `keep_slots`: the entries of a row are distinct patch indices of the image; the first visible_count of them are its visible patches, the others are ignored.
All inputs are finite; a program needn't handle non-finite values.
Results may differ from a plain program's by a relative error of at most 0.012.
The roundings to bfloat16 on the way count: a program that leaves them out, or rounds other values in their place, can miss the bound.
Values may be sent and summed in bfloat16 or wider, within the bound.
No kernel may reach another device: no remote copies, remote signals or barrier semaphores. Data moves between devices by JAX's collectives and lax.ppermute only.
A program may use at most 192 MiB of HBM per device.

v0:
```python
import jax
import jax.numpy as jnp
from jax import lax
from jax.sharding import PartitionSpec as P

HD = 64
EPSILON = 1e-06
MASKED = -1000000000.0


def standard(inputs):
    average = jnp.mean(inputs, axis=-1, keepdims=True)
    centered = inputs - average
    spread = jnp.mean(centered * centered, axis=-1, keepdims=True)
    return centered * lax.rsqrt(spread + EPSILON)


def affine_norm(inputs, weights, offsets):
    return standard(inputs) * weights + offsets


def norm_back(inputs, weights, offsets, gradient):
    _, backward = jax.vjp(affine_norm, inputs, weights, offsets)
    return backward(gradient)


def exact_gelu(values):
    return jax.nn.gelu(values, approximate=False)


def shards(
    patches,
    keep_slots,
    visible_count,
    gain_one,
    shift_one,
    w_qkv,
    b_qv,
    w_out,
    b_out,
    gain_two,
    shift_two,
    w_fc1,
    b_fc1,
    w_fc2,
    b_fc2,
    out_grad,
):
    images, slots = keep_slots.shape
    share = images // lax.axis_size("tensor")
    begin = lax.axis_index("tensor") * share
    visible = jnp.arange(slots, dtype=jnp.int32)[None, :] < visible_count[:, None]
    mask_share = lax.dynamic_slice_in_dim(visible, begin, share, 0)[:, :, None].astype(jnp.float32)
    tokens = jnp.take_along_axis(patches, keep_slots[:, :, None], axis=1).astype(jnp.float32)
    token_share = lax.dynamic_slice_in_dim(tokens, begin, share, 0)
    first = affine_norm(tokens, gain_one, shift_one).astype(jnp.bfloat16)
    projected = jnp.einsum("ivd,sdh->sivh", first, w_qkv, preferred_element_type=jnp.float32)
    local_heads = w_qkv.shape[2] // HD
    heads_shape = (images, slots, local_heads, HD)
    queries = (projected[0] + b_qv[0]).astype(jnp.bfloat16).reshape(heads_shape)
    keyset = projected[1].astype(jnp.bfloat16).reshape(heads_shape)
    valueset = (projected[2] + b_qv[1]).astype(jnp.bfloat16).reshape(heads_shape)
    factor = HD ** (-0.5)
    key_visible = visible[:, None, None, :]

    def scores_of(query_part, key_part):
        raw_scores = (
            jnp.einsum("iqhe,ikhe->ihqk", query_part, key_part, preferred_element_type=jnp.float32)
            * factor
        )
        return jnp.where(key_visible, raw_scores, MASKED)

    scores = scores_of(queries, keyset)
    highest = jnp.max(scores, axis=-1, keepdims=True)
    logsum = highest + jnp.log(jnp.sum(jnp.exp(scores - highest), axis=-1, keepdims=True))
    attention = jnp.exp(scores - logsum).astype(jnp.bfloat16)
    attended = jnp.einsum(
        "ihqk,ikhe->iqhe", attention, valueset, preferred_element_type=jnp.float32
    )
    attended = attended.astype(jnp.bfloat16).reshape(images, slots, local_heads * HD)
    branch_part = jnp.einsum("ivc,cd->ivd", attended, w_out, preferred_element_type=jnp.float32)
    middle = tokens + lax.psum(branch_part, "tensor") + b_out
    middle_share = lax.dynamic_slice_in_dim(middle, begin, share, 0)
    second = affine_norm(middle, gain_two, shift_two).astype(jnp.bfloat16)
    inner = jnp.einsum("ivd,df->ivf", second, w_fc1, preferred_element_type=jnp.float32) + b_fc1
    hidden_values, gelu_back = jax.vjp(exact_gelu, inner)
    hidden = hidden_values.astype(jnp.bfloat16)
    mlp_part = jnp.einsum("ivf,fd->ivd", hidden, w_fc2, preferred_element_type=jnp.float32)
    mlp_share = lax.psum_scatter(
        mlp_part.astype(jnp.bfloat16), "tensor", scatter_dimension=0, tiled=True
    ).astype(jnp.float32)
    layer_out = ((middle_share + mlp_share + b_fc2) * mask_share).astype(jnp.bfloat16)
    grad_share = out_grad.astype(jnp.float32) * mask_share
    grad_b_fc2 = jnp.sum(grad_share, axis=(0, 1))
    grad_rows = lax.all_gather(grad_share.astype(jnp.bfloat16), "tensor", axis=0, tiled=True)
    grad_w_fc2 = jnp.einsum("ivf,ivd->fd", hidden, grad_rows, preferred_element_type=jnp.float32)
    grad_hidden = jnp.einsum("ivd,fd->ivf", grad_rows, w_fc2, preferred_element_type=jnp.float32)
    grad_inner = gelu_back(grad_hidden)[0].astype(jnp.bfloat16)
    grad_b_fc1 = jnp.sum(grad_inner, axis=(0, 1), dtype=jnp.float32)
    grad_w_fc1 = jnp.einsum("ivd,ivf->df", second, grad_inner, preferred_element_type=jnp.float32)
    second_part = jnp.einsum("ivf,df->ivd", grad_inner, w_fc1, preferred_element_type=jnp.float32)
    grad_second = lax.psum(second_part, "tensor")
    _, middle_back = jax.vjp(lambda inputs: affine_norm(inputs, gain_two, shift_two), middle)
    grad_middle = grad_rows.astype(jnp.float32) + middle_back(grad_second)[0]
    grad_second_share = lax.dynamic_slice_in_dim(grad_second, begin, share, 0)
    grad_gain_two = jnp.sum(grad_second_share * standard(middle_share), axis=(0, 1))
    grad_shift_two = jnp.sum(grad_second_share, axis=(0, 1))
    grad_middle_share = lax.dynamic_slice_in_dim(grad_middle, begin, share, 0)
    grad_middle_rows = grad_middle.astype(jnp.bfloat16)
    grad_b_out = jnp.sum(grad_middle_share, axis=(0, 1))
    grad_w_out = jnp.einsum(
        "ivc,ivd->cd", attended, grad_middle_rows, preferred_element_type=jnp.float32
    )
    grad_attended = jnp.einsum(
        "ivd,cd->ivc", grad_middle_rows, w_out, preferred_element_type=jnp.float32
    )
    grad_attended = grad_attended.astype(jnp.bfloat16).reshape(heads_shape)
    again = scores_of(queries, keyset)
    prob_exact = jnp.exp(again - logsum)
    prob_round = prob_exact.astype(jnp.bfloat16)
    grad_prob = jnp.einsum(
        "iqhe,ikhe->ihqk", grad_attended, valueset, preferred_element_type=jnp.float32
    )
    grad_scores = prob_exact * (grad_prob - jnp.sum(prob_exact * grad_prob, axis=-1, keepdims=True))
    grad_scores = grad_scores.astype(jnp.bfloat16)
    grad_queries = (
        jnp.einsum("ihqk,ikhe->iqhe", grad_scores, keyset, preferred_element_type=jnp.float32)
        * factor
    ).astype(jnp.bfloat16)
    grad_keys = (
        jnp.einsum("ihqk,iqhe->ikhe", grad_scores, queries, preferred_element_type=jnp.float32)
        * factor
    ).astype(jnp.bfloat16)
    grad_values = jnp.einsum(
        "ihqk,iqhe->ikhe", prob_round, grad_attended, preferred_element_type=jnp.float32
    ).astype(jnp.bfloat16)
    grad_projected = jnp.stack([grad_queries, grad_keys, grad_values]).reshape(
        3, images, slots, local_heads * HD
    )
    grad_b_qv = jnp.stack(
        [
            jnp.sum(grad_projected[0], axis=(0, 1), dtype=jnp.float32),
            jnp.sum(grad_projected[2], axis=(0, 1), dtype=jnp.float32),
        ]
    )
    grad_w_qkv = jnp.einsum(
        "ivd,sivh->sdh", first, grad_projected, preferred_element_type=jnp.float32
    )
    first_part = jnp.einsum(
        "sivh,sdh->ivd", grad_projected, w_qkv, preferred_element_type=jnp.float32
    )
    grad_first_share = lax.psum_scatter(first_part, "tensor", scatter_dimension=0, tiled=True)
    token_grad, grad_gain_one, grad_shift_one = norm_back(
        token_share, gain_one, shift_one, grad_first_share
    )
    grad_tokens = grad_middle_share + token_grad
    slot_share = lax.dynamic_slice_in_dim(keep_slots, begin, share, 0)
    image_rows = jnp.arange(share, dtype=jnp.int32)[:, None]
    grad_patches = (
        jnp.zeros((share, patches.shape[1], patches.shape[2]), jnp.float32)
        .at[image_rows, slot_share]
        .add(grad_tokens)
    )
    grad_w_qkv, grad_b_qv, grad_w_out, grad_w_fc1, grad_b_fc1, grad_w_fc2 = lax.psum(
        (grad_w_qkv, grad_b_qv, grad_w_out, grad_w_fc1, grad_b_fc1, grad_w_fc2), "dp"
    )
    grad_gain_one, grad_shift_one, grad_b_out, grad_gain_two, grad_shift_two, grad_b_fc2 = lax.psum(
        (grad_gain_one, grad_shift_one, grad_b_out, grad_gain_two, grad_shift_two, grad_b_fc2),
        ("dp", "tensor"),
    )
    return (
        layer_out,
        grad_patches,
        grad_gain_one,
        grad_shift_one,
        grad_w_qkv,
        grad_b_qv,
        grad_w_out,
        grad_b_out,
        grad_gain_two,
        grad_shift_two,
        grad_w_fc1,
        grad_b_fc1,
        grad_w_fc2,
        grad_b_fc2,
    )


def solution(mesh):
    return jax.shard_map(
        shards,
        mesh=mesh,
        in_specs=(
            P("dp", None, None),
            P("dp", None),
            P("dp"),
            P(),
            P(),
            P(None, None, "tensor"),
            P(None, "tensor"),
            P("tensor", None),
            P(),
            P(),
            P(),
            P(None, "tensor"),
            P("tensor"),
            P("tensor", None),
            P(),
            P(("dp", "tensor"), None, None),
        ),
        out_specs=(
            P(("dp", "tensor"), None, None),
            P(("dp", "tensor"), None, None),
            P(),
            P(),
            P(None, None, "tensor"),
            P(None, "tensor"),
            P("tensor", None),
            P(),
            P(),
            P(),
            P(None, "tensor"),
            P("tensor"),
            P("tensor", None),
            P(),
        ),
        check_vma=False,
    )
```

profile of v0, /device:TPU:0, one launch (start us, length us, event | category | flops | bytes accessed | tf_op | source)
XLA Modules:
  0.0 807.6 jit_solution(15770494399392824385)
XLA Ops:
  8.9 41.4 %gather_fusion = bf16[2352,768]{1,0:T(8,128)(2,1)} fusion(bf16[24,196,768]{2,0,1:T(8,128)(2,1)} %param.16, s32[2352]{0:T(1024)S(1)} %reshape.192), kind=kCustom, calls=%fused_computation | custom fusion | bytes 7244160 | tf_op jit(solution)/shard_map/jit(take_along_axis)/gather | solution.py:54
  50.3 5.8 reshape.195
  56.1 3.0 convert_reduce_fusion.3
  59.4 2.1 multiply_reduce_fusion.2
  61.6 3.3 convolution_bitcast_fusion.1
  64.9 1.8 fusion.58
  70.1 2.7 fusion.7
  74.3 1.6 copy-done.10
  78.4 4.3 fusion.36
  83.1 3.0 fusion.14
  86.2 141.4 %all-reduce.7.cloned.1.call-done = f32[24,98,768]{2,1,0:T(8,128)} async-done(((f32[24,98,768]{2,1,0:T(8,128)}), f32[24,98,768]{2,1,0:T(8,128)}) %all-reduce.7.cloned.1.call-update) | async-done | bytes 7225360 | tf_op jit(solution)/shard_map/psum | solution.py:82
  227.6 5.3 fusion.57
  236.0 6.4 convert_reduce_fusion.1
  242.5 3.0 copy-done.16
  245.5 18.4 %multiply_convert_fusion = (bf16[24,98,768]{2,1,0:T(8,128)(2,1)}, f32[24,98,768]{2,1,0:T(8,128)}) fusion(f32[24,98,768]{2,1,0:T(8,128)S(1)} %get-tuple-element.52, f32[768]{0:T(1024)S(1)} %copy-done.56, u32[98,768]{1,0:T(8,128)S(1)} %get-tuple-element.19, u32[98,768]{1,0:T(8,128)S(1)} %get-tuple-element.18), kind=kLoop, calls=%fused_computation.14 | loop fusion | flops 124637184 | bytes 18668544 | tf_op jit(solution)/shard_map/convert_element_type | solution.py:87
  263.9 11.6 %convert_reduce_fusion.2 = (f32[768]{0:T(1024)}, bf16[24,98,768]{2,1,0:T(8,128)(2,1)S(1)}) fusion(f32[24,98,768]{2,1,0:T(8,128)} %get-tuple-element.38, bf16[24,98,768]{2,1,0:T(8,128)(2,1)} %all-gather.2.cloned.1.call-done, bf16[768,768]{1,0:T(8,128)(2,1)} %param.29, f32[24,98,768]{2,1,0:T(8,128)} %copy-done.16, f32[768]{0:T(1024)} %param.28), kind=kOutput, calls=%fused_computation.10 | convolution fusion | flops 2805239040 | bytes 22861824 | tf_op jit(solution)/shard_map/ivd,fd->ivf/dot_general | solution.py:97
  275.5 1.8 copy-done.65
  277.3 15.7 %fusion.24 = f32[24,98,768]{2,1,0:T(8,128)} fusion(bf16[24,98,768]{2,1,0:T(8,128)(2,1)S(1)} %get-tuple-element.60, bf16[768,768]{1,0:T(8,128)(2,1)S(1)} %copy-done), kind=kOutput, calls=%fused_computation.83 | convolution fusion | flops 2774532096 | bytes 12017664 | tf_op jit(solution)/shard_map/ivf,df->ivd/dot_general | solution.py:101
  294.4 7.1 convolution_convert_fusion
  301.6 133.9 %all-reduce.9.cloned.1.call-done = f32[24,98,768]{2,1,0:T(8,128)} async-done(((f32[24,98,768]{2,1,0:T(8,128)}), f32[24,98,768]{2,1,0:T(8,128)}) %all-reduce.9.cloned.1.call-update) | async-done | bytes 7225360 | tf_op jit(solution)/shard_map/psum | solution.py:102
  435.5 6.4 multiply_reduce_fusion
  443.1 6.5 fusion.28
  450.6 2.9 add_add_fusion.1
  453.6 1.6 fusion.16
  455.2 2.3 copy-done.8
  459.2 2.1 multiply_reduce_fusion.3
  465.6 1.9 convert_reduce_fusion.4
  467.5 5.4 convolution_bitcast_fusion
  473.3 8.2 %convolution_bitcast_fusion.2 = f32[768,768]{1,0:T(8,128)} fusion(bf16[24,98,768]{2,1,0:T(8,128)(2,1)} %get-tuple-element.37, bf16[24,98,768]{2,1,0:T(8,128)(2,1)} %all-gather.2.cloned.1.call-done), kind=kOutput, calls=%fused_computation.73 | convolution fusion | flops 2774532096 | bytes 9584640 | tf_op jit(solution)/shard_map/ivf,ivd->fd/dot_general | solution.py:96
  481.5 8.8 %convolution_bitcast_fusion.3 = f32[768,768]{1,0:T(8,128)} fusion(bf16[24,98,768]{2,1,0:T(8,128)(2,1)S(1)} %copy-done.66, f32[24,98,768]{2,1,0:T(8,128)} %copy-done.2, f32[768]{0:T(1024)S(1)} %copy-done.62, f32[768]{0:T(1024)S(1)} %copy-done.42, f32[24,98]{1,0:T(8,128)S(1)} %copy-done.33, f32[24,98]{1,0:T(8,128)S(1)} %broadcast_multiply_fusion), kind=kOutput, calls=%fused_computation.74 | convolution fusion | flops 2783563776 | bytes 13222272 | tf_op jit(solution)/shard_map/ivd,ivf->df/dot_general | solution.py:100
  490.4 1.9 fusion.19
  494.9 5.7 convolution_bitcast_fusion.4
  501.4 2.7 fusion.9
  504.1 3.8 copy-done.9
  508.2 1.7 dynamic-slice_reduce_fusion.3
  509.9 1.9 multiply_reduce_fusion.5
  512.0 22.0 %all-reduce.1 = (f32[2,192]{1,0:T(2,128)}, f32[768]{0:T(1024)}) all-reduce(f32[2,192]{1,0:T(2,128)S(1)} %pad_maximum_fusion.3, f32[768]{0:T(1024)S(1)} %copy-done.58), channel_id=1, replica_groups=mesh['dp'=8,'tensor'=4] {'dp'}, use_global_device_ids=true, to_apply=%region_25.26 | all-reduce | flops 1152 | bytes 9216 | tf_op jit(solution)/shard_map/psum | solution.py:164
  534.0 3.9 dynamic-slice_reduce_fusion
  537.9 12.8 %reduce-scatter.5.cloned.1.call-done = f32[6,98,768]{2,1,0:T(8,128)} async-done(((f32[24,98,768]{2,1,0:T(8,128)}), f32[6,98,768]{2,1,0:T(8,128)}) %reduce-scatter.5.cloned.1.call-update) | async-done | bytes 1806352 | tf_op jit(solution)/shard_map/reduce_scatter | solution.py:152
  550.8 2.9 multiply_reduce_fusion.8
  553.7 2.4 multiply_reduce_fusion.6
  556.1 4.0 dynamic-slice_reduce_fusion.2
  560.2 1.6 reshape.200
  561.8 2.1 broadcast_in_dim.42
  564.0 81.2 %scatter_fusion = f32[6,196,768]{2,1,0:T(8,128)} fusion(f32[6,196,768]{2,1,0:T(8,128)} %broadcast_in_dim.42, s32[588]{0:T(1024)S(1)} %reshape.198, f32[588,768]{1,0:T(8,128)S(1)} %reshape.200), kind=kCustom, calls=%fused_computation.1 | custom fusion | flops 451584 | bytes 5423712 | tf_op jit(solution)/shard_map/scatter-add | solution.py:162
  645.2 41.1 %all-reduce = (f32[768]{0:T(1024)}, f32[768]{0:T(1024)}, f32[768]{0:T(1024)}, f32[768]{0:T(1024)}, f32[768]{0:T(1024)}, /*index=5*/f32[768]{0:T(1024)}) all-reduce(f32[768]{0:T(1024)S(1)} %get-tuple-element.14, f32[768]{0:T(1024)S(1)} %get-tuple-element.22, ...), channel_id=1, replica_groups=mesh['dp'=8,'tensor'=4] {'dp','tensor'}, use_global_device_ids=true, to_apply=%region_19.20 | all-reduce | flops 4608 | bytes 36864 | tf_op jit(solution)/shard_map/psum | solution.py:167
  686.3 107.5 %all-reduce.11.cloned.1.call-done = (f32[3,768,192]{1,2,0:T(8,128)}, f32[192,768]{1,0:T(8,128)}, f32[768,768]{1,0:T(8,128)}, f32[768,768]{1,0:T(8,128)}) async-done(((f32[3,768,192]{1,2,0:T(8,128)}, f32[192,768]{1,0:T(8,128)}, f32[768,768]{1,0:T(8,128)}, f32[768,768]{1,0:T(8,128)}), (f32[3,768,192]{1,2,0:T(8,128)}, f32[192,768]{1,0:T(8,128)}, f32[768,768]{1,0:T(8,128)}, ...) | async-done | bytes 7077904 | tf_op jit(solution)/shard_map/psum | solution.py:164
  793.8 2.9 copy.66
  (189 shorter events, 29.8 us)
Async XLA Ops:
  7.2 228.8 %copy-start = (bf16[768,768]{1,0:T(8,128)(2,1)S(1)}, bf16[768,768]{1,0:T(8,128)(2,1)}, u32[]{:S(2)}) copy-start(bf16[768,768]{1,0:T(8,128)(2,1)} %param.27) | copy-start | bytes 3538948
  7.2 220.4 %all-reduce.7.cloned.1.call-start = ((), (), s32[]{:S(2)}) async-start(), calls=%async_computation.2 | async-start | bytes 15335424 | tf_op jit(solution)/shard_map/psum | solution.py:82
  8.8 218.8 %copy-start.36 = (pred[24,98]{1,0:T(8,128)(4,1)}, pred[24,98]{1,0:T(8,128)(4,1)S(1)}, u32[]{:S(2)}) copy-start(pred[24,98]{1,0:T(8,128)(4,1)S(1)} %compare_and_fusion) | copy-start | bytes 7060
  56.1 5.4 copy-start.26
  56.1 5.4 copy-start.45
  56.1 5.4 copy-start.63
  59.4 5.5 copy-start.38
  68.6 5.7 copy-start.49
  70.1 4.1 copy-start.47
  72.8 4.5 copy-start.5
  74.2 4.2 copy-start.24
  82.7 144.8 %copy-start.55 = (f32[768]{0:T(1024)S(1)}, f32[768]{0:T(1024)}, u32[]{:S(2)}) copy-start(f32[768]{0:T(1024)} %param.24) | copy-start | bytes 9220
  82.7 181.2 %all-gather.2.cloned.1.call-start = ((), (), s32[]{:S(2)}) async-start(), calls=%async_computation.4 | async-start | bytes 4792320 | tf_op jit(solution)/shard_map/all_gather | solution.py:95
  83.1 149.8 %copy-start.43 = (f32[6,98]{1,0:T(8,128)}, f32[6,98]{1,0:T(8,128)S(1)}, u32[]{:S(2)}) copy-start(f32[6,98]{1,0:T(8,128)S(1)} %dynamic-slice_convert_fusion) | copy-start | bytes 7060
  86.1 349.4 %all-reduce.9.cloned.1.call-start = ((), (), s32[]{:S(2)}) async-start(), calls=%async_computation.5 | async-start | bytes 15335424 | tf_op jit(solution)/shard_map/psum | solution.py:102
  236.0 6.5 copy-start.31
  293.1 240.9 %reduce-scatter.3.cloned.1.call-start = ((), (), s32[]{:S(2)}) async-start(), calls=%async_computation.3 | async-start | bytes 4792320 | tf_op jit(solution)/shard_map/reduce_scatter | solution.py:89
  301.5 134.0 %copy-start.41 = (f32[768]{0:T(1024)S(1)}, f32[768]{0:T(1024)}, u32[]{:S(2)}) copy-start(f32[768]{0:T(1024)} %param.25) | copy-start | bytes 9220
  301.5 140.4 %copy-start.35 = (f32[24,98]{1,0:T(8,128)S(1)}, f32[24,98]{1,0:T(8,128)}, u32[]{:S(2)}) copy-start(f32[24,98]{1,0:T(8,128)} %copy-done.34) | copy-start | bytes 28228
  301.5 140.4 %copy-start.32 = (f32[24,98]{1,0:T(8,128)S(1)}, f32[24,98]{1,0:T(8,128)}, u32[]{:S(2)}) copy-start(f32[24,98]{1,0:T(8,128)} %copy-done.31) | copy-start | bytes 28228
  301.5 249.2 %reduce-scatter.5.cloned.1.call-start = ((), (), s32[]{:S(2)}) async-start(), calls=%async_computation.6 | async-start | bytes 9584640 | tf_op jit(solution)/shard_map/reduce_scatter | solution.py:152
  435.5 7.6 copy-start.7
  435.5 14.1 %slice-start = ((s8[7667712]{0:T(1024)(128)(4,1)}), s8[4194304]{0:T(1024)(128)(4,1)S(1)}, s32[]{:S(2)}) async-start(s8[7667712]{0:T(1024)(128)(4,1)} %bitcast.93), calls=%async_computation.8 | async-start | bytes 8388608
  443.1 6.5 slice-start.1
  443.1 7.5 copy-start.21
  453.5 4.9 copy-start.6
  453.5 5.7 copy-start.11
  453.5 5.6 copy-start.29
  453.6 5.6 copy-start.50
  465.5 7.4 copy-start.17
  473.0 8.5 %copy-start.33 = (f32[24,98]{1,0:T(8,128)S(1)}, f32[24,98]{1,0:T(8,128)}, u32[]{:S(2)}) copy-start(f32[24,98]{1,0:T(8,128)} %copy-done.31) | copy-start | bytes 28228
  473.0 8.5 %copy-start.42 = (f32[768]{0:T(1024)S(1)}, f32[768]{0:T(1024)}, u32[]{:S(2)}) copy-start(f32[768]{0:T(1024)} %param.25) | copy-start | bytes 9220
  473.0 8.5 %copy-start.62 = (f32[768]{0:T(1024)S(1)}, f32[768]{0:T(1024)}, u32[]{:S(2)}) copy-start(f32[768]{0:T(1024)} %param.26) | copy-start | bytes 9220
  473.0 320.7 %all-reduce.11.cloned.1.call-start = ((), (), s32[]{:S(2)}) async-start(), calls=%async_computation.7 | async-start | bytes 14155776 | tf_op jit(solution)/shard_map/psum | solution.py:164
  473.3 8.2 %copy-start.66 = (bf16[24,98,768]{2,1,0:T(8,128)(2,1)S(1)}, bf16[24,98,768]{2,1,0:T(8,128)(2,1)}, u32[]{:S(2)}) copy-start(bf16[24,98,768]{2,1,0:T(8,128)(2,1)} %copy-done.65) | copy-start | bytes 10838020
  473.3 17.0 %slice-start.2 = ((s8[7667712]{0:T(1024)(128)(4,1)}), s8[4194304]{0:T(1024)(128)(4,1)S(1)}, s32[]{:S(2)}) async-start(s8[7667712]{0:T(1024)(128)(4,1)} %bitcast.95), calls=%async_computation.10 | async-start | bytes 8388608
  481.5 8.8 %slice-start.3 = ((s8[7667712]{0:T(1024)(128)(4,1)}), s8[3473408]{0:T(1024)(128)(4,1)S(1)}, s32[]{:S(2)}) async-start(s8[7667712]{0:T(1024)(128)(4,1)} %bitcast.95), calls=%async_computation.11 | async-start | bytes 6946816
  481.5 8.8 %copy-start.14 = (bf16[24,3,64,98]{3,2,1,0:T(8,128)(2,1)S(1)}, bf16[24,3,64,98]{3,2,1,0:T(8,128)(2,1)}, u32[]{:S(2)}) copy-start(bf16[24,3,64,98]{3,2,1,0:T(8,128)(2,1)} %copy-done.13) | copy-start | bytes 2709508
  490.4 4.5 copy-start.20
  490.4 4.5 copy-start.37
  490.4 4.5 copy-start.39
  490.4 4.5 copy-start.46
  490.4 4.5 copy-start.53
  490.4 4.5 copy-start.64
  507.9 26.0 %copy-start.44 = (f32[6,98]{1,0:T(8,128)S(1)}, f32[6,98]{1,0:T(8,128)}, u32[]{:S(2)}) copy-start(f32[6,98]{1,0:T(8,128)} %copy-done.43) | copy-start | bytes 7060
  507.9 26.0 %copy-start.57 = (f32[768]{0:T(1024)S(1)}, f32[768]{0:T(1024)}, u32[]{:S(2)}) copy-start(f32[768]{0:T(1024)} %param.30) | copy-start | bytes 9220
  563.9 81.2 %copy-start.51 = (f32[768]{0:T(1024)S(1)}, f32[768]{0:T(1024)}, u32[]{:S(2)}) copy-start(f32[768]{0:T(1024)} %get-tuple-element.46) | copy-start | bytes 9220
  793.8 5.2 copy-start.22
  (29 other events, 83.6 us)
Sparse Core Ops, SparseCore 0:
  82.9 144.6 all-reduce.6
  229.8 32.6 all-gather.1
  293.2 142.2 all-reduce.8
  437.9 42.5 reduce-scatter.2
  483.0 67.6 reduce-scatter.4
  556.2 237.5 all-reduce.10
where the time goes:
time: 820 us; the launch traced here: 808 us
  waiting for transfers between devices  396 us (48%)
  other arithmetic  156 us (19%)
  matrix products  91 us (11%)
  local copies, waits for them, and re-layouts  85.9 us (10%)
  blocking collectives  63.1 us (8%)
  between operations  15.4 us (2%)
    psum x1, waiting for transfers between devices, shards(): middle = tokens + lax.psum(branch_part, 'tensor') + b_out  141 us
    psum x1, waiting for transfers between devices, shards(): grad_second = lax.psum(second_part, 'tensor')  134 us
    psum x1, waiting for transfers between devices, shards(): lax.psum((grad_w_qkv, grad_b_qv, grad_w_out, grad_w_fc1, grad_b_fc1, grad...  107 us
    scatter-add x1, other arithmetic, shards(): grad_patches = jnp.zeros((share, patches.shape[1], patches.shape[2]), jnp...  81.2 us
    gather x3, local copies, waits for them, and re-layouts, shards(): jnp.take_along_axis(patches, keep_slots[:, :, None], axis=1)  47.4 us
    psum x1, blocking collectives, shards(): lax.psum((grad_gain_one, grad_shift_one, grad_b_out, grad_gain_two, grad_...  41.1 us
    unnamed x146, local copies, waits for them, and re-layouts  30.1 us
    psum x1, blocking collectives, shards(): lax.psum((grad_w_qkv, grad_b_qv, grad_w_out, grad_w_fc1, grad_b_fc1, grad...  22 us
  transfers between devices with their start and end apart: 6, of which 4 were waited for; matrix products, arithmetic and copies ran while one was open for 25% of the time, Pallas kernels for 0%

commit v1 on v0

--- a/solution.py
+++ b/solution.py
@@ -99,7 +99,11 @@
     grad_b_fc1 = jnp.sum(grad_inner, axis=(0, 1), dtype=jnp.float32)
     grad_w_fc1 = jnp.einsum("ivd,ivf->df", second, grad_inner, preferred_element_type=jnp.float32)
     second_part = jnp.einsum("ivf,df->ivd", grad_inner, w_fc1, preferred_element_type=jnp.float32)
-    grad_second = lax.psum(second_part, "tensor")
+    grad_second = second_part
+    for hop in (1, 2):
+        grad_second = grad_second + lax.ppermute(
+            grad_second, "tensor", [(dev, dev ^ hop) for dev in range(4)]
+        )
     _, middle_back = jax.vjp(lambda inputs: affine_norm(inputs, gain_two, shift_two), middle)
     grad_middle = grad_rows.astype(jnp.float32) + middle_back(grad_second)[0]
     grad_second_share = lax.dynamic_slice_in_dim(grad_second, begin, share, 0)

time: 820 us -> 871 us (1.062)
  waiting for transfers between devices: 396 us -> 437 us
  other arithmetic: 156 us -> 171 us
  matrix products: 91 us -> 80.2 us
    ppermute x0 -> x2, waiting for transfers between devices: none -> 185 us  [shards(): lax.ppermute(grad_second, 'tensor', [(dev, dev ^ hop) for dev in range(4)])]
    psum x1 -> x0, waiting for transfers between devices: 134 us -> none  [shards(): grad_second = lax.psum(second_part, 'tensor')]
    dot_general x1, matrix products: 15.7 us -> 3.22 us  [shards(): jnp.einsum('ivf,df->ivd', grad_inner, w_fc1, preferred_element_type=jnp.f...]
    reduce_scatter x1, waiting for transfers between devices: 12.8 us -> 3.52 us  [shards(): lax.psum_scatter(first_part, 'tensor', scatter_dimension=0, tiled=True)]
  transfers between devices with their start and end apart: 6 -> 7, of which waited for: 4 -> 5; matrix products, arithmetic and copies ran while one was open for 25% -> 24% of each run, Pallas kernels for 0% -> 0%
where the time goes in v1:
time: 871 us; the launch traced here: 858 us
  waiting for transfers between devices  437 us (50%)
  other arithmetic  171 us (20%)
  local copies, waits for them, and re-layouts  90 us (10%)
  matrix products  80.2 us (9%)
  blocking collectives  63.5 us (7%)
  between operations  14.9 us (2%)
    ppermute x2, waiting for transfers between devices, shards(): lax.ppermute(grad_second, 'tensor', [(dev, dev ^ hop) for dev in range(4)])  185 us
    psum x1, waiting for transfers between devices, shards(): middle = tokens + lax.psum(branch_part, 'tensor') + b_out  141 us
    psum x1, waiting for transfers between devices, shards(): lax.psum((grad_w_qkv, grad_b_qv, grad_w_out, grad_w_fc1, grad_b_fc1, grad...  108 us
    scatter-add x1, other arithmetic, shards(): grad_patches = jnp.zeros((share, patches.shape[1], patches.shape[2]), jnp...  81.2 us
    gather x3, local copies, waits for them, and re-layouts, shards(): jnp.take_along_axis(patches, keep_slots[:, :, None], axis=1)  47.4 us
    psum x1, blocking collectives, shards(): lax.psum((grad_gain_one, grad_shift_one, grad_b_out, grad_gain_two, grad_...  41.2 us
    unnamed x146, local copies, waits for them, and re-layouts  26.4 us
    psum x1, blocking collectives, shards(): lax.psum((grad_w_qkv, grad_b_qv, grad_w_out, grad_w_fc1, grad_b_fc1, grad...  22.2 us
  transfers between devices with their start and end apart: 7, of which 5 were waited for; matrix products, arithmetic and copies ran while one was open for 24% of the time, Pallas kernels for 0%

profile of v1, /device:TPU:0, one launch (start us, length us, event | category | flops | bytes accessed | tf_op | source)
XLA Modules:
  0.0 858.3 jit_solution(10286286334301651477)
XLA Ops:
  8.9 41.4 %gather_fusion = bf16[2352,768]{1,0:T(8,128)(2,1)} fusion(bf16[24,196,768]{2,0,1:T(8,128)(2,1)} %param.16, s32[2352]{0:T(1024)S(1)} %reshape.192), kind=kCustom, calls=%fused_computation | custom fusion | bytes 7244160 | tf_op jit(solution)/shard_map/jit(take_along_axis)/gather | solution.py:54
  50.3 5.9 reshape.195
  56.2 3.0 convert_reduce_fusion.3
  59.4 2.1 multiply_reduce_fusion.2
  61.6 3.3 convolution_bitcast_fusion.1
  69.4 2.7 fusion.7
  72.1 1.9 copy-done.5
  76.1 4.1 convolution_convert_fusion.2
  81.2 4.3 fusion.36
  86.1 3.0 fusion.14
  89.2 141.2 %all-reduce.6.cloned.1.call-done = f32[24,98,768]{2,1,0:T(8,128)} async-done(((f32[24,98,768]{2,1,0:T(8,128)}), f32[24,98,768]{2,1,0:T(8,128)}) %all-reduce.6.cloned.1.call-update) | async-done | bytes 7225360 | tf_op jit(solution)/shard_map/psum | solution.py:82
  230.4 5.3 fusion.57
  238.8 6.4 convert_reduce_fusion.1
  245.3 3.0 copy-done.17
  248.3 18.5 %multiply_convert_fusion = (bf16[24,98,768]{2,1,0:T(8,128)(2,1)}, f32[24,98,768]{2,1,0:T(8,128)}) fusion(f32[24,98,768]{2,1,0:T(8,128)S(1)} %get-tuple-element.54, f32[768]{0:T(1024)S(1)} %copy-done.57, u32[98,768]{1,0:T(8,128)S(1)} %get-tuple-element.19, u32[98,768]{1,0:T(8,128)S(1)} %get-tuple-element.18), kind=kLoop, calls=%fused_computation.16 | loop fusion | flops 124637184 | bytes 18668544 | tf_op jit(solution)/shard_map/convert_element_type | solution.py:87
  266.8 11.8 %convert_reduce_fusion.2 = (f32[768]{0:T(1024)}, bf16[24,98,768]{2,1,0:T(8,128)(2,1)S(1)}) fusion(f32[24,98,768]{2,1,0:T(8,128)} %get-tuple-element.40, bf16[24,98,768]{2,1,0:T(8,128)(2,1)} %all-gather.2.cloned.1.call-done, bf16[768,768]{1,0:T(8,128)(2,1)} %param.29, f32[24,98,768]{2,1,0:T(8,128)} %copy-done.17, f32[768]{0:T(1024)} %param.28), kind=kOutput, calls=%fused_computation.12 | convolution fusion | flops 2805239040 | bytes 22861824 | tf_op jit(solution)/shard_map/ivd,fd->ivf/dot_general | solution.py:97
  280.4 3.2 fusion.24
  283.7 2.3 copy.47
  286.8 11.6 %collective-permute-done = f32[24,98,768]{2,0,1:T(8,128)} collective-permute-done((f32[24,98,768]{2,0,1:T(8,128)S(1)}, f32[24,98,768]{2,0,1:T(8,128)}, u32[]{:S(2)}, u32[]{:S(2)}) %collective-permute-start) | collective-permute-done | bytes 7225376 | tf_op jit(solution)/shard_map/ppermute | solution.py:104
  298.4 7.8 copy_add_fusion.1
  306.2 5.5 copy.49
  313.4 4.6 convolution_convert_fusion
  318.0 173.2 %collective-permute-done.1 = f32[24,98,768]{2,0,1:T(8,128)} collective-permute-done((f32[24,98,768]{2,0,1:T(8,128)}, f32[24,98,768]{2,0,1:T(8,128)}, u32[]{:S(2)}, u32[]{:S(2)}) %collective-permute-start.1) | collective-permute-done | bytes 7225376 | tf_op jit(solution)/shard_map/ppermute | solution.py:104
  491.2 9.5 %multiply_reduce_fusion = (f32[24,98]{1,0:T(8,128)S(1)}, f32[24,98,768]{2,1,0:T(8,128)S(1)}) fusion(f32[24,98,768]{2,1,0:T(8,128)} %copy-done.2, f32[768]{0:T(1024)S(1)} %copy-done.46, f32[24,98]{1,0:T(8,128)S(1)} %broadcast_multiply_fusion, f32[24,98,768]{2,1,0:T(8,128)} %copy-done.9, f32[24,98,768]{2,0,1:T(8,128)} %collective-permute-done.1), kind=kLoop, calls=%fused_computation.14 | loop fusion | flops 9029328 | bytes 28923264 | tf_op jit(solution)/shard_map/transpose(jvp())/reduce_sum | solution.py:15
  500.8 7.6 fusion.28
  508.5 5.5 add_add_fusion.1
  515.6 2.2 copy-done.7
  519.5 2.1 multiply_reduce_fusion.3
  525.9 2.0 convert_reduce_fusion.4
  527.9 5.4 convolution_bitcast_fusion
  533.9 8.1 convolution_bitcast_fusion.2
  542.0 10.3 %convolution_bitcast_fusion.3 = f32[768,768]{1,0:T(8,128)} fusion(bf16[24,98,768]{2,1,0:T(8,128)(2,1)S(1)} %copy-done.68, f32[24,98,768]{2,1,0:T(8,128)} %copy-done.2, f32[768]{0:T(1024)S(1)} %copy-done.64, f32[768]{0:T(1024)S(1)} %copy-done.47, f32[24,98]{1,0:T(8,128)S(1)} %copy-done.34, f32[24,98]{1,0:T(8,128)S(1)} %broadcast_multiply_fusion), kind=kOutput, calls=%fused_computation.76 | convolution fusion | flops 2783563776 | bytes 13222272 | tf_op jit(solution)/shard_map/ivd,ivf->df/dot_general | solution.py:100
  552.4 1.9 fusion.19
  555.4 5.7 convolution_bitcast_fusion.4
  561.9 2.6 fusion.9
  564.5 3.1 copy-done.10
  569.6 2.0 multiply_reduce_fusion.5
  571.8 22.2 %all-reduce.1 = (f32[2,192]{1,0:T(2,128)}, f32[768]{0:T(1024)}) all-reduce(f32[2,192]{1,0:T(2,128)S(1)} %pad_maximum_fusion.3, f32[768]{0:T(1024)S(1)} %copy-done.59), channel_id=1, replica_groups=mesh['dp'=8,'tensor'=4] {'dp'}, use_global_device_ids=true, to_apply=%region_24.25 | all-reduce | flops 1152 | bytes 9216 | tf_op jit(solution)/shard_map/psum | solution.py:168
  594.0 3.9 dynamic-slice_reduce_fusion
  598.0 3.5 reduce-scatter.5.cloned.1.call-done
  601.5 2.9 multiply_reduce_fusion.8
  604.4 2.4 multiply_reduce_fusion.6
  606.9 4.0 dynamic-slice_reduce_fusion.2
  612.5 2.1 broadcast_in_dim.42
  614.6 81.2 %scatter_fusion = f32[6,196,768]{2,1,0:T(8,128)} fusion(f32[6,196,768]{2,1,0:T(8,128)} %broadcast_in_dim.42, s32[588]{0:T(1024)S(1)} %reshape.198, f32[588,768]{1,0:T(8,128)S(1)} %reshape.200), kind=kCustom, calls=%fused_computation.1 | custom fusion | flops 451584 | bytes 5423712 | tf_op jit(solution)/shard_map/scatter-add | solution.py:166
  695.8 41.2 %all-reduce = (f32[768]{0:T(1024)}, f32[768]{0:T(1024)}, f32[768]{0:T(1024)}, f32[768]{0:T(1024)}, f32[768]{0:T(1024)}, /*index=5*/f32[768]{0:T(1024)}) all-reduce(f32[768]{0:T(1024)S(1)} %get-tuple-element.14, f32[768]{0:T(1024)S(1)} %get-tuple-element.22, ...), channel_id=1, replica_groups=mesh['dp'=8,'tensor'=4] {'dp','tensor'}, use_global_device_ids=true, to_apply=%region_18.19 | all-reduce | flops 4608 | bytes 36864 | tf_op jit(solution)/shard_map/psum | solution.py:171
  737.1 107.9 %all-reduce.8.cloned.1.call-done = (f32[3,768,192]{1,2,0:T(8,128)}, f32[192,768]{1,0:T(8,128)}, f32[768,768]{1,0:T(8,128)}, f32[768,768]{1,0:T(8,128)}) async-done(((f32[3,768,192]{1,2,0:T(8,128)}, f32[192,768]{1,0:T(8,128)}, f32[768,768]{1,0:T(8,128)}, f32[768,768]{1,0:T(8,128)}), (f32[3,768,192]{1,2,0:T(8,128)}, f32[192,768]{1,0:T(8,128)}, f32[768,768]{1,0:T(8,128)}, ...) | async-done | bytes 7077904 | tf_op jit(solution)/shard_map/psum | solution.py:168
  845.0 2.9 copy.72
  (192 shorter events, 34.6 us)
Async XLA Ops:
  7.2 231.6 %copy-start = (bf16[768,768]{1,0:T(8,128)(2,1)S(1)}, bf16[768,768]{1,0:T(8,128)(2,1)}, u32[]{:S(2)}) copy-start(bf16[768,768]{1,0:T(8,128)(2,1)} %param.27) | copy-start | bytes 3538948
  7.2 223.2 %all-reduce.6.cloned.1.call-start = ((), (), s32[]{:S(2)}) async-start(), calls=%async_computation.2 | async-start | bytes 15335424 | tf_op jit(solution)/shard_map/psum | solution.py:82
  8.8 221.6 %copy-start.37 = (pred[24,98]{1,0:T(8,128)(4,1)}, pred[24,98]{1,0:T(8,128)(4,1)S(1)}, u32[]{:S(2)}) copy-start(pred[24,98]{1,0:T(8,128)(4,1)S(1)} %compare_and_fusion) | copy-start | bytes 7060
  56.1 5.4 copy-start.28
  56.1 5.4 copy-start.43
  56.1 5.4 copy-start.65
  59.4 5.5 copy-start.39
  69.4 6.0 copy-start.48
  76.1 9.4 %copy-start.50 = (f32[3,64]{1,0:T(4,128)}, f32[3,64]{1,0:T(4,128)S(1)}, u32[]{:S(2)}) copy-start(f32[3,64]{1,0:T(4,128)S(1)} %add.186) | copy-start | bytes 2308
  76.1 5.1 copy-start.26
  85.5 144.8 %copy-start.56 = (f32[768]{0:T(1024)S(1)}, f32[768]{0:T(1024)}, u32[]{:S(2)}) copy-start(f32[768]{0:T(1024)} %param.24) | copy-start | bytes 9220
  85.6 181.3 %all-gather.2.cloned.1.call-start = ((), (), s32[]{:S(2)}) async-start(), calls=%async_computation.4 | async-start | bytes 4792320 | tf_op jit(solution)/shard_map/all_gather | solution.py:95
  86.1 149.6 %copy-start.41 = (f32[6,98]{1,0:T(8,128)}, f32[6,98]{1,0:T(8,128)S(1)}, u32[]{:S(2)}) copy-start(f32[6,98]{1,0:T(8,128)S(1)} %dynamic-slice_convert_fusion) | copy-start | bytes 7060
  89.2 504.9 %reduce-scatter.3.cloned.1.call-start = ((), (), s32[]{:S(2)}) async-start(), calls=%async_computation.3 | async-start | bytes 4792320 | tf_op jit(solution)/shard_map/reduce_scatter | solution.py:89
  238.8 6.5 copy-start.32
  286.8 11.6 %collective-permute-start = (f32[24,98,768]{2,0,1:T(8,128)S(1)}, f32[24,98,768]{2,0,1:T(8,128)}, u32[]{:S(2)}, u32[]{:S(2)}) collective-permute-start(f32[24,98,768]{2,0,1:T(8,128)S(1)} %copy.47), channel_id=1, source_target_pairs={{0,1},{1,0},{2,3},{3,2},{4,5},{5,4},{6,7},{7,6},{8,9},{9,8},{10,11... | collective-permute-start | bytes 21676040 | tf_op jit(solution)/shard_map/ppermute | solution.py:104
  306.2 6.5 copy-start.9
  306.2 7.1 copy-start.23
  306.2 7.1 copy-start.62
  312.8 178.4 %collective-permute-start.1 = (f32[24,98,768]{2,0,1:T(8,128)}, f32[24,98,768]{2,0,1:T(8,128)}, u32[]{:S(2)}, u32[]{:S(2)}) collective-permute-start(f32[24,98,768]{2,0,1:T(8,128)} %copy.49), channel_id=1, source_target_pairs={{0,2},{1,3},{2,0},{3,1},{4,6},{5,7},{6,4},{7,5},{8,10},{9,11},{10,... | collective-permute-start | bytes 21676040 | tf_op jit(solution)/shard_map/ppermute | solution.py:104
  317.9 173.3 %copy-start.46 = (f32[768]{0:T(1024)S(1)}, f32[768]{0:T(1024)}, u32[]{:S(2)}) copy-start(f32[768]{0:T(1024)} %param.25) | copy-start | bytes 9220
  318.0 182.8 %copy-start.36 = (f32[24,98]{1,0:T(8,128)S(1)}, f32[24,98]{1,0:T(8,128)}, u32[]{:S(2)}) copy-start(f32[24,98]{1,0:T(8,128)} %copy-done.35) | copy-start | bytes 28228
  318.0 182.8 %copy-start.33 = (f32[24,98]{1,0:T(8,128)S(1)}, f32[24,98]{1,0:T(8,128)}, u32[]{:S(2)}) copy-start(f32[24,98]{1,0:T(8,128)} %copy-done.32) | copy-start | bytes 28228
  318.0 283.5 %reduce-scatter.5.cloned.1.call-start = ((), (), s32[]{:S(2)}) async-start(), calls=%async_computation.5 | async-start | bytes 9584640 | tf_op jit(solution)/shard_map/reduce_scatter | solution.py:156
  500.7 7.7 copy-start.8
  500.8 7.7 copy-start.22
  508.5 5.5 copy-start.27
  513.9 3.9 copy-start.7
  514.0 4.9 copy-start.6
  514.0 5.6 copy-start.12
  514.0 5.6 copy-start.30
  514.0 5.6 copy-start.51
  525.9 7.4 copy-start.18
  533.4 8.6 %copy-start.34 = (f32[24,98]{1,0:T(8,128)S(1)}, f32[24,98]{1,0:T(8,128)}, u32[]{:S(2)}) copy-start(f32[24,98]{1,0:T(8,128)} %copy-done.32) | copy-start | bytes 28228
  533.4 8.6 copy-start.47
  533.4 8.6 copy-start.64
  533.4 311.6 %all-reduce.8.cloned.1.call-start = ((), (), s32[]{:S(2)}) async-start(), calls=%async_computation.6 | async-start | bytes 14155776 | tf_op jit(solution)/shard_map/psum | solution.py:168
  533.9 8.1 copy-start.68
  533.9 18.5 %slice-start = ((s8[7667712]{0:T(1024)(128)(4,1)}), s8[4194304]{0:T(1024)(128)(4,1)S(1)}, s32[]{:S(2)}) async-start(s8[7667712]{0:T(1024)(128)(4,1)} %bitcast.93), calls=%async_computation.7 | async-start | bytes 8388608
  542.0 10.4 %slice-start.1 = ((s8[7667712]{0:T(1024)(128)(4,1)}), s8[3473408]{0:T(1024)(128)(4,1)S(1)}, s32[]{:S(2)}) async-start(s8[7667712]{0:T(1024)(128)(4,1)} %bitcast.93), calls=%async_computation.8 | async-start | bytes 6946816
  542.0 10.4 %copy-start.15 = (bf16[24,3,64,98]{3,2,1,0:T(8,128)(2,1)S(1)}, bf16[24,3,64,98]{3,2,1,0:T(8,128)(2,1)}, u32[]{:S(2)}) copy-start(bf16[24,3,64,98]{3,2,1,0:T(8,128)(2,1)} %copy-done.14) | copy-start | bytes 2709508
  567.6 3.9 copy-start.55
  567.6 4.1 copy-start.59
  567.6 26.4 %copy-start.42 = (f32[6,98]{1,0:T(8,128)S(1)}, f32[6,98]{1,0:T(8,128)}, u32[]{:S(2)}) copy-start(f32[6,98]{1,0:T(8,128)} %copy-done.41) | copy-start | bytes 7060
  567.6 26.4 %copy-start.58 = (f32[768]{0:T(1024)S(1)}, f32[768]{0:T(1024)}, u32[]{:S(2)}) copy-start(f32[768]{0:T(1024)} %param.30) | copy-start | bytes 9220
  614.6 81.2 %copy-start.52 = (f32[768]{0:T(1024)S(1)}, f32[768]{0:T(1024)}, u32[]{:S(2)}) copy-start(f32[768]{0:T(1024)} %get-tuple-element.48) | copy-start | bytes 9220
  845.0 3.8 copy-start.25
  845.0 5.2 copy-start.24
  (30 other events, 80.2 us)
Sparse Core Ops, SparseCore 0:
  85.7 144.6 all-reduce.5
  232.6 32.6 all-gather.1
  318.1 63.7 reduce-scatter.2
  533.5 67.9 reduce-scatter.4
  607.5 237.4 all-reduce.7
